TPU v7x, 256 devices: a whole 4x4x8 slice. The times are simulated.
256 devices in a mesh: layer: 2 (over z_lo), row: 8 (over y, core), col: 16 (over z_hi, x).
Axes of the slice: x: 4, y: 4, z: 8 (z_hi: 4, z_lo: 2; z = z_hi * 2 + z_lo), core: 2. Of those that a mesh axis runs over, the one named last changes fastest.
Arguments:
- matrix: float32 [16384, 16384], P('row', 'col'), may hold values from -1.5 to 1.5, as said below
Outputs:
- square_panel: float32 [16384, 512], P('row', 'layer')
- new_panel: float32 [16384, 512], P('row', 'layer')
Inputs may be any that keep to these rules, and one draw needn't show every extreme that they name: `matrix`: entries off the diagonal are of order 0.5 / sqrt(16384); the diagonal's magnitudes lie between 0.6 and 1 with either sign.
All inputs are finite; a program needn't handle non-finite values.
Results may differ from a plain program's by a relative error of at most 0.000076.
Values sent between devices are 32-bit elements; how exact they have to be, the bound alone decides.
A program may use at most 128 MiB of HBM per device.

v0:
```python
import jax
import jax.numpy as jnp
from jax import lax
from jax.sharding import PartitionSpec as P

PW = 512


def from_root(shard, axis, root):
    mine = lax.axis_index(axis) == root
    return lax.psum(jnp.where(mine, shard, jnp.zeros_like(shard)), axis)


def matmul_high(left_side, right_side):
    return jnp.dot(
        left_side, right_side, precision=lax.Precision.HIGHEST, preferred_element_type=jnp.float32
    )


def body(matrix):
    block_cols = matrix.shape[1]
    layers = lax.axis_size("layer")
    col_ratio = lax.axis_size("col") // lax.axis_size("row")
    col_index = lax.axis_index("col")
    layer_index = lax.axis_index("layer")
    half_width = PW // layers
    root_row = col_index // col_ratio
    offset = col_index % col_ratio * block_cols
    panel_full = from_root(matrix[:, :PW], "col", 0)
    own_cols = lax.dynamic_slice_in_dim(panel_full, layer_index * half_width, half_width, 1)
    depth_rows = block_cols // layers
    first_row = offset + layer_index * depth_rows
    panel_slab = from_root(
        lax.dynamic_slice_in_dim(panel_full, first_row, depth_rows, 0), "row", root_row
    )
    local_cols = lax.dynamic_slice_in_dim(matrix, layer_index * depth_rows, depth_rows, 1)
    square_full = lax.psum(matmul_high(local_cols, panel_slab), ("layer", "col"))
    square_slab = from_root(
        lax.dynamic_slice_in_dim(square_full, first_row, depth_rows, 0), "row", root_row
    )
    update = lax.psum_scatter(
        matmul_high(local_cols, square_slab), "layer", scatter_dimension=1, tiled=True
    )
    update = lax.psum(update, "col")
    square = lax.dynamic_slice_in_dim(square_full, layer_index * half_width, half_width, 1)
    new_panel = (3.0 * own_cols - update) * 0.5
    return (square, new_panel)


def solution(mesh):
    placed = (P("row", "col"),)
    return jax.shard_map(
        body,
        mesh=mesh,
        in_specs=placed,
        out_specs=(P("row", "layer"), P("row", "layer")),
        check_vma=False,
    )
```

profile of v0, /device:TPU:16, one launch (start us, length us, event | category | flops | bytes accessed | tf_op | source)
XLA Modules:
  0.0 809.4 jit_solution(460881230599396828)
XLA Ops:
  7.2 0.0 all-reduce.6.cloned.1.call-start
  7.2 4.6 slice_select_fusion
  11.9 0.0 all-reduce.6.cloned.1.call-update
  11.9 0.0 all-reduce.8.cloned.1.call-start
  12.0 224.7 %all-reduce.6.cloned.1.call-done = f32[2048,512]{1,0:T(8,128)} async-done(((f32[2048,512]{1,0:T(8,128)}), f32[2048,512]{1,0:T(8,128)}) %all-reduce.6.cloned.1.call-update) | async-done | bytes 4194320 | tf_op jit(solution)/shard_map/psum | solution.py:11
  236.6 2.3 dynamic-slice_select_fusion.1
  238.9 0.0 all-reduce.8.cloned.1.call-update
  239.0 0.0 all-reduce.10.cloned.1.call-start
  239.0 61.4 %all-reduce.8.cloned.1.call-done = f32[512,512]{1,0:T(8,128)} async-done(((f32[512,512]{1,0:T(8,128)}), f32[512,512]{1,0:T(8,128)}) %all-reduce.8.cloned.1.call-update) | async-done | bytes 1048592 | tf_op jit(solution)/shard_map/psum | solution.py:11
  300.4 10.1 %fusion.2 = f32[2048,512]{1,0:T(8,128)} fusion(f32[512,512]{1,0:T(8,128)} %all-reduce.8.cloned.1.call-done, f32[2048,1024]{1,0:T(8,128)} %param.1, s32[]{:T(128)S(6)} %select_n.42), kind=kOutput, calls=%fused_computation.3 | convolution fusion | flops 6442450944 | bytes 9437188 | tf_op jit(solution)/shard_map/dot_general | solution.py:15
  310.5 0.0 all-reduce.10.cloned.1.call-update
  310.5 0.0 all-reduce.12.cloned.1.call-start
  310.6 167.7 %all-reduce.10.cloned.1.call-done = f32[2048,512]{1,0:T(8,128)} async-done(((f32[2048,512]{1,0:T(8,128)}), f32[2048,512]{1,0:T(8,128)}) %all-reduce.10.cloned.1.call-update) | async-done | bytes 4194320 | tf_op jit(solution)/shard_map/psum | solution.py:37
  478.2 2.3 dynamic-slice_select_fusion
  480.5 0.0 all-reduce.12.cloned.1.call-update
  480.6 0.0 reduce-scatter.2.cloned.1.call-start
  480.6 61.5 %all-reduce.12.cloned.1.call-done = f32[512,512]{1,0:T(8,128)} async-done(((f32[512,512]{1,0:T(8,128)}), f32[512,512]{1,0:T(8,128)}) %all-reduce.12.cloned.1.call-update) | async-done | bytes 1048592 | tf_op jit(solution)/shard_map/psum | solution.py:11
  542.1 10.1 %fusion = f32[2048,512]{1,0:T(8,128)} fusion(f32[512,512]{1,0:T(8,128)} %all-reduce.12.cloned.1.call-done, f32[2048,1024]{1,0:T(8,128)} %param.1, s32[]{:T(128)S(6)} %select_n.42), kind=kOutput, calls=%fused_computation.1 | convolution fusion | flops 6442450944 | bytes 9437188 | tf_op jit(solution)/shard_map/dot_general | solution.py:15
  552.2 0.0 reduce-scatter.2.cloned.1.call-update
  552.2 0.0 all-reduce.14.cloned.1.call-start
  552.2 62.9 %reduce-scatter.2.cloned.1.call-done = f32[2048,256]{1,0:T(8,128)} async-done(((f32[2048,512]{1,0:T(8,128)}), f32[2048,256]{1,0:T(8,128)}) %reduce-scatter.2.cloned.1.call-update) | async-done | bytes 2097168 | tf_op jit(solution)/shard_map/reduce_scatter | solution.py:41
  615.2 0.0 all-reduce.14.cloned.1.call-update
  615.2 3.0 constant_dynamic-slice_fusion
  618.3 180.5 %all-reduce.14.cloned.1.call-done = f32[2048,256]{1,0:T(8,128)} async-done(((f32[2048,256]{1,0:T(8,128)}), f32[2048,256]{1,0:T(8,128)}) %all-reduce.14.cloned.1.call-update) | async-done | bytes 2097168 | tf_op jit(solution)/shard_map/psum | solution.py:44
  798.7 3.8 subtract_multiply_fusion
Async XLA Ops:
  7.2 229.5 %all-reduce.6.cloned.1.call-start = ((), (), s32[]{:S(2)}) async-start(), calls=%async_computation.1 | async-start | bytes 8388608 | tf_op jit(solution)/shard_map/psum | solution.py:11
  11.9 288.5 %all-reduce.8.cloned.1.call-start = ((), (), s32[]{:S(2)}) async-start(), calls=%async_computation.2 | async-start | bytes 2097152 | tf_op jit(solution)/shard_map/psum | solution.py:11
  239.0 239.3 %all-reduce.10.cloned.1.call-start = ((), (), s32[]{:S(2)}) async-start(), calls=%async_computation.3 | async-start | bytes 8388608 | tf_op jit(solution)/shard_map/psum | solution.py:37
  310.5 231.6 %all-reduce.12.cloned.1.call-start = ((), (), s32[]{:S(2)}) async-start(), calls=%async_computation.4 | async-start | bytes 2097152 | tf_op jit(solution)/shard_map/psum | solution.py:11
  480.6 134.6 %reduce-scatter.2.cloned.1.call-start = ((), (), s32[]{:S(2)}) async-start(), calls=%async_computation.5 | async-start | bytes 6291456 | tf_op jit(solution)/shard_map/reduce_scatter | solution.py:41
  552.2 246.5 %all-reduce.14.cloned.1.call-start = ((), (), s32[]{:S(2)}) async-start(), calls=%async_computation.6 | async-start | bytes 4194304 | tf_op jit(solution)/shard_map/psum | solution.py:44
Sparse Core Ops, SparseCore 0:
  12.0 224.5 all-reduce.5
  239.6 60.7 all-reduce.7
  310.6 167.5 all-reduce.9
  481.0 61.0 all-reduce.11
  552.3 62.8 reduce-scatter.1
  617.7 180.9 all-reduce.13
where the time goes:
time: 810 us; the launch traced here: 809 us
  waiting for transfers between devices  759 us (94%)
  matrix products  20.1 us (2%)
  between operations  14.2 us (2%)
  other arithmetic  13 us (2%)
    psum x3, waiting for transfers between devices, from_root(): return lax.psum(jnp.where(mine, shard, jnp.zeros_like(shard)), axis)  348 us
    psum x1, waiting for transfers between devices, body(): update = lax.psum(update, 'col')  180 us
    psum x1, waiting for transfers between devices, body(): lax.psum(matmul_high(local_cols, panel_slab), ('layer', 'col'))  168 us
    reduce_scatter x1, waiting for transfers between devices, body(): lax.psum_scatter(matmul_high(local_cols, square_slab), 'layer', scatter_d...  62.9 us
    dot_general x2, matrix products, matmul_high(): jnp.dot(left_side, right_side, precision=lax.Precision.HIGHEST, preferred...  20.1 us
  transfers between devices with their start and end apart: 6, of which 6 were waited for; matrix products, arithmetic and copies ran while one was open for 0% of the time, Pallas kernels for 0%

commit v1 on v0

--- a/solution.py
+++ b/solution.py
@@ -1,9 +1,18 @@
+import functools
 import jax
 import jax.numpy as jnp
 from jax import lax
 from jax.sharding import PartitionSpec as P
 
 PW = 512
+
+
+def settle_record(inp, ax_name, dev_axis):
+    side_arr = lax.psum(inp, ax_name)
+    return lax.psum(side_arr, dev_axis)
+
+
+part_keys = functools.partial(settle_record, ax_name="layer", dev_axis="col")
 
 
 def from_root(shard, axis, root):
@@ -34,7 +43,7 @@
         lax.dynamic_slice_in_dim(panel_full, first_row, depth_rows, 0), "row", root_row
     )
     local_cols = lax.dynamic_slice_in_dim(matrix, layer_index * depth_rows, depth_rows, 1)
-    square_full = lax.psum(matmul_high(local_cols, panel_slab), ("layer", "col"))
+    square_full = part_keys(matmul_high(local_cols, panel_slab))
     square_slab = from_root(
         lax.dynamic_slice_in_dim(square_full, first_row, depth_rows, 0), "row", root_row
     )

time: 810 us -> 990 us (1.22)
  waiting for transfers between devices: 759 us -> 938 us
    psum x1 -> x2, waiting for transfers between devices: 168 us -> 348 us  [the longest x1 225 us: settle_record(): return lax.psum(side_arr, dev_axis)]
  transfers between devices with their start and end apart: 6 -> 7, of which waited for: 6 -> 7; matrix products, arithmetic and copies ran while one was open for 0% -> 0% of each run, Pallas kernels for 0% -> 0%
where the time goes in v1:
time: 990 us; the launch traced here: 989 us
  waiting for transfers between devices  938 us (95%)
  matrix products  20.2 us (2%)
  between operations  14.2 us (1%)
  other arithmetic  13 us (1%)
    psum x3, waiting for transfers between devices, from_root(): return lax.psum(jnp.where(mine, shard, jnp.zeros_like(shard)), axis)  347 us
    psum x1, waiting for transfers between devices, settle_record(): return lax.psum(side_arr, dev_axis)  225 us
    psum x1, waiting for transfers between devices, body(): update = lax.psum(update, 'col')  180 us
    psum x1, waiting for transfers between devices, settle_record(): side_arr = lax.psum(inp, ax_name)  123 us
    reduce_scatter x1, waiting for transfers between devices, body(): lax.psum_scatter(matmul_high(local_cols, square_slab), 'layer', scatter_d...  62.9 us
    dot_general x2, matrix products, matmul_high(): jnp.dot(left_side, right_side, precision=lax.Precision.HIGHEST, preferred...  20.2 us
  transfers between devices with their start and end apart: 7, of which 7 were waited for; matrix products, arithmetic and copies ran while one was open for 0% of the time, Pallas kernels for 0%

profile of v1, /device:TPU:16, one launch (start us, length us, event | category | flops | bytes accessed | tf_op | source)
XLA Modules:
  0.0 989.0 jit_solution(5295545514116654973)
XLA Ops:
  7.2 0.0 all-reduce.7.cloned.1.call-start
  7.2 4.6 slice_select_fusion
  11.9 0.0 all-reduce.7.cloned.1.call-update
  11.9 0.0 all-reduce.9.cloned.1.call-start
  12.0 224.7 %all-reduce.7.cloned.1.call-done = f32[2048,512]{1,0:T(8,128)} async-done(((f32[2048,512]{1,0:T(8,128)}), f32[2048,512]{1,0:T(8,128)}) %all-reduce.7.cloned.1.call-update) | async-done | bytes 4194320 | tf_op jit(solution)/shard_map/psum | solution.py:20
  236.6 2.3 dynamic-slice_select_fusion.1
  238.9 0.0 all-reduce.9.cloned.1.call-update
  239.0 0.0 all-reduce.11.cloned.1.call-start
  239.0 61.4 %all-reduce.9.cloned.1.call-done = f32[512,512]{1,0:T(8,128)} async-done(((f32[512,512]{1,0:T(8,128)}), f32[512,512]{1,0:T(8,128)}) %all-reduce.9.cloned.1.call-update) | async-done | bytes 1048592 | tf_op jit(solution)/shard_map/psum | solution.py:20
  300.4 10.1 %fusion.2 = f32[2048,512]{1,0:T(8,128)} fusion(f32[512,512]{1,0:T(8,128)} %all-reduce.9.cloned.1.call-done, f32[2048,1024]{1,0:T(8,128)} %param.1, s32[]{:T(128)S(6)} %select_n.42), kind=kOutput, calls=%fused_computation.3 | convolution fusion | flops 6442450944 | bytes 9437188 | tf_op jit(solution)/shard_map/dot_general | solution.py:24
  310.5 0.0 all-reduce.11.cloned.1.call-update
  310.5 0.0 all-reduce.13.cloned.1.call-start
  310.6 122.6 %all-reduce.11.cloned.1.call-done = f32[2048,512]{1,0:T(8,128)} async-done(((f32[2048,512]{1,0:T(8,128)}), f32[2048,512]{1,0:T(8,128)}) %all-reduce.11.cloned.1.call-update) | async-done | bytes 4194320 | tf_op jit(solution)/shard_map/psum | solution.py:11
  433.2 0.0 all-reduce.13.cloned.1.call-update
  433.2 0.0 all-reduce.15.cloned.1.call-start
  433.3 225.3 %all-reduce.13.cloned.1.call-done = f32[2048,512]{1,0:T(8,128)} async-done(((f32[2048,512]{1,0:T(8,128)}), f32[2048,512]{1,0:T(8,128)}) %all-reduce.13.cloned.1.call-update) | async-done | bytes 4194320 | tf_op jit(solution)/shard_map/psum | solution.py:12
  658.6 2.3 dynamic-slice_select_fusion
  660.8 0.0 all-reduce.15.cloned.1.call-update
  660.9 0.0 reduce-scatter.2.cloned.1.call-start
  660.9 61.3 %all-reduce.15.cloned.1.call-done = f32[512,512]{1,0:T(8,128)} async-done(((f32[512,512]{1,0:T(8,128)}), f32[512,512]{1,0:T(8,128)}) %all-reduce.15.cloned.1.call-update) | async-done | bytes 1048592 | tf_op jit(solution)/shard_map/psum | solution.py:20
  722.2 10.1 %fusion = f32[2048,512]{1,0:T(8,128)} fusion(f32[512,512]{1,0:T(8,128)} %all-reduce.15.cloned.1.call-done, f32[2048,1024]{1,0:T(8,128)} %param.1, s32[]{:T(128)S(6)} %select_n.42), kind=kOutput, calls=%fused_computation.1 | convolution fusion | flops 6442450944 | bytes 9437188 | tf_op jit(solution)/shard_map/dot_general | solution.py:24
  732.2 0.0 reduce-scatter.2.cloned.1.call-update
  732.3 0.0 all-reduce.17.cloned.1.call-start
  732.3 62.9 %reduce-scatter.2.cloned.1.call-done = f32[2048,256]{1,0:T(8,128)} async-done(((f32[2048,512]{1,0:T(8,128)}), f32[2048,256]{1,0:T(8,128)}) %reduce-scatter.2.cloned.1.call-update) | async-done | bytes 2097168 | tf_op jit(solution)/shard_map/reduce_scatter | solution.py:50
  795.3 0.0 all-reduce.17.cloned.1.call-update
  795.3 3.0 constant_dynamic-slice_fusion
  798.3 180.0 %all-reduce.17.cloned.1.call-done = f32[2048,256]{1,0:T(8,128)} async-done(((f32[2048,256]{1,0:T(8,128)}), f32[2048,256]{1,0:T(8,128)}) %all-reduce.17.cloned.1.call-update) | async-done | bytes 2097168 | tf_op jit(solution)/shard_map/psum | solution.py:53
  978.4 3.8 subtract_multiply_fusion
Async XLA Ops:
  7.2 229.5 %all-reduce.7.cloned.1.call-start = ((), (), s32[]{:S(2)}) async-start(), calls=%async_computation.1 | async-start | bytes 8388608 | tf_op jit(solution)/shard_map/psum | solution.py:20
  11.9 288.5 %all-reduce.9.cloned.1.call-start = ((), (), s32[]{:S(2)}) async-start(), calls=%async_computation.2 | async-start | bytes 2097152 | tf_op jit(solution)/shard_map/psum | solution.py:20
  239.0 194.2 %all-reduce.11.cloned.1.call-start = ((), (), s32[]{:S(2)}) async-start(), calls=%async_computation.3 | async-start | bytes 8388608 | tf_op jit(solution)/shard_map/psum | solution.py:11
  310.5 348.0 %all-reduce.13.cloned.1.call-start = ((), (), s32[]{:S(2)}) async-start(), calls=%async_computation.4 | async-start | bytes 8388608 | tf_op jit(solution)/shard_map/psum | solution.py:12
  433.2 289.0 %all-reduce.15.cloned.1.call-start = ((), (), s32[]{:S(2)}) async-start(), calls=%async_computation.5 | async-start | bytes 2097152 | tf_op jit(solution)/shard_map/psum | solution.py:20
  660.9 134.4 %reduce-scatter.2.cloned.1.call-start = ((), (), s32[]{:S(2)}) async-start(), calls=%async_computation.6 | async-start | bytes 6291456 | tf_op jit(solution)/shard_map/reduce_scatter | solution.py:50
  732.3 246.1 %all-reduce.17.cloned.1.call-start = ((), (), s32[]{:S(2)}) async-start(), calls=%async_computation.7 | async-start | bytes 4194304 | tf_op jit(solution)/shard_map/psum | solution.py:53
Sparse Core Ops, SparseCore 0:
  12.0 224.5 all-reduce.6
  239.6 60.7 all-reduce.8
  310.7 122.4 all-reduce.10
  435.7 222.7 all-reduce.12
  661.3 60.7 all-reduce.14
  732.4 62.8 reduce-scatter.1
  797.9 180.4 all-reduce.16

commit v2 on v0

--- a/solution.py
+++ b/solution.py
@@ -4,6 +4,11 @@
 from jax.sharding import PartitionSpec as P
 
 PW = 512
+
+
+def gather_and_add(x, axis):
+    parts = lax.all_gather(x, axis)
+    return jnp.sum(parts, axis=0)
 
 
 def from_root(shard, axis, root):
@@ -41,7 +46,7 @@
     update = lax.psum_scatter(
         matmul_high(local_cols, square_slab), "layer", scatter_dimension=1, tiled=True
     )
-    update = lax.psum(update, "col")
+    update = gather_and_add(update, "col")
     square = lax.dynamic_slice_in_dim(square_full, layer_index * half_width, half_width, 1)
     new_panel = (3.0 * own_cols - update) * 0.5
     return (square, new_panel)

time: 810 us -> 1010 us (1.25)
  waiting for transfers between devices: 759 us -> 951 us
  other arithmetic: 13 us -> 24.5 us
    all_gather x0 -> x1, waiting for transfers between devices: none -> 373 us  [gather_and_add(): parts = lax.all_gather(x, axis)]
    psum x1 -> x0, waiting for transfers between devices: 180 us -> none  [body(): update = lax.psum(update, 'col')]
    reduce_sum x0 -> x1, other arithmetic: none -> 12.1 us  [gather_and_add(): return jnp.sum(parts, axis=0)]
where the time goes in v2:
time: 1010 us
  waiting for transfers between devices  951 us (94%)
  other arithmetic  24.5 us (2%)
  matrix products  20.1 us (2%)
  between operations  14.2 us (1%)
    all_gather x1, waiting for transfers between devices, gather_and_add(): parts = lax.all_gather(x, axis)  373 us
    psum x3, waiting for transfers between devices, from_root(): return lax.psum(jnp.where(mine, shard, jnp.zeros_like(shard)), axis)  348 us
    psum x1, waiting for transfers between devices, body(): lax.psum(matmul_high(local_cols, panel_slab), ('layer', 'col'))  168 us
    reduce_scatter x1, waiting for transfers between devices, body(): lax.psum_scatter(matmul_high(local_cols, square_slab), 'layer', scatter_d...  62.9 us
  transfers between devices with their start and end apart: 6, of which 6 were waited for; matrix products, arithmetic and copies ran while one was open for 0% of the time, Pallas kernels for 0%

profile of v2, /device:TPU:16, one launch (start us, length us, event | category | flops | bytes accessed | tf_op | source)
XLA Modules:
  0.0 1013.3 jit_solution(9647460425007924038)
XLA Ops:
  7.2 0.0 all-reduce.5.cloned.1.call-start
  7.2 4.6 slice_select_fusion
  11.8 0.0 all-reduce.5.cloned.1.call-update
  11.9 0.0 all-reduce.7.cloned.1.call-start
  11.9 224.7 %all-reduce.5.cloned.1.call-done = f32[2048,512]{1,0:T(8,128)} async-done(((f32[2048,512]{1,0:T(8,128)}), f32[2048,512]{1,0:T(8,128)}) %all-reduce.5.cloned.1.call-update) | async-done | bytes 4194320 | tf_op jit(solution)/shard_map/psum | solution.py:16
  236.6 2.3 dynamic-slice_select_fusion.1
  238.9 0.0 all-reduce.7.cloned.1.call-update
  238.9 0.0 all-reduce.9.cloned.1.call-start
  239.0 61.4 %all-reduce.7.cloned.1.call-done = f32[512,512]{1,0:T(8,128)} async-done(((f32[512,512]{1,0:T(8,128)}), f32[512,512]{1,0:T(8,128)}) %all-reduce.7.cloned.1.call-update) | async-done | bytes 1048592 | tf_op jit(solution)/shard_map/psum | solution.py:16
  300.4 10.1 fusion.2
  310.4 0.0 all-reduce.9.cloned.1.call-update
  310.5 0.0 all-reduce.11.cloned.1.call-start
  310.5 167.7 %all-reduce.9.cloned.1.call-done = f32[2048,512]{1,0:T(8,128)} async-done(((f32[2048,512]{1,0:T(8,128)}), f32[2048,512]{1,0:T(8,128)}) %all-reduce.9.cloned.1.call-update) | async-done | bytes 4194320 | tf_op jit(solution)/shard_map/psum | solution.py:42
  478.2 2.3 dynamic-slice_select_fusion
  480.5 0.0 all-reduce.11.cloned.1.call-update
  480.5 0.0 reduce-scatter.2.cloned.1.call-start
  480.5 61.5 %all-reduce.11.cloned.1.call-done = f32[512,512]{1,0:T(8,128)} async-done(((f32[512,512]{1,0:T(8,128)}), f32[512,512]{1,0:T(8,128)}) %all-reduce.11.cloned.1.call-update) | async-done | bytes 1048592 | tf_op jit(solution)/shard_map/psum | solution.py:16
  542.0 10.1 fusion
  552.1 0.0 reduce-scatter.2.cloned.1.call-update
  552.1 0.0 all-gather.3.cloned.1.call-start
  552.2 62.9 %reduce-scatter.2.cloned.1.call-done = f32[2048,256]{1,0:T(8,128)} async-done(((f32[2048,512]{1,0:T(8,128)}), f32[2048,256]{1,0:T(8,128)}) %reduce-scatter.2.cloned.1.call-update) | async-done | bytes 2097168 | tf_op jit(solution)/shard_map/reduce_scatter | solution.py:46
  615.1 0.0 all-gather.3.cloned.1.call-update
  615.2 3.0 constant_dynamic-slice_fusion
  618.2 373.0 %all-gather.3.cloned.1.call-done = f32[32768,256]{1,0:T(8,128)} async-done(((f32[2048,256]{1,0:T(8,128)}), f32[32768,256]{1,0:T(8,128)}) %all-gather.3.cloned.1.call-update) | async-done | bytes 33554448 | tf_op jit(solution)/shard_map/all_gather | solution.py:10
  991.2 12.1 %reduce_sum.9 = f32[2048,256]{1,0:T(8,128)S(1)} reduce(f32[16,2048,256]{2,1,0:T(8,128)} %bitcast.3, f32[]{:T(128)} %constant.49.clone.1), dimensions={0}, to_apply=%region_5.6 | reduce | flops 7864320 | bytes 35651588 | tf_op jit(solution)/shard_map/reduce_sum | solution.py:11
  1003.3 3.2 subtract_multiply_fusion
Async XLA Ops:
  7.2 229.5 %all-reduce.5.cloned.1.call-start = ((), (), s32[]{:S(2)}) async-start(), calls=%async_computation.1 | async-start | bytes 8388608 | tf_op jit(solution)/shard_map/psum | solution.py:16
  11.9 288.5 %all-reduce.7.cloned.1.call-start = ((), (), s32[]{:S(2)}) async-start(), calls=%async_computation.2 | async-start | bytes 2097152 | tf_op jit(solution)/shard_map/psum | solution.py:16
  238.9 239.3 %all-reduce.9.cloned.1.call-start = ((), (), s32[]{:S(2)}) async-start(), calls=%async_computation.3 | async-start | bytes 8388608 | tf_op jit(solution)/shard_map/psum | solution.py:42
  310.5 231.6 %all-reduce.11.cloned.1.call-start = ((), (), s32[]{:S(2)}) async-start(), calls=%async_computation.4 | async-start | bytes 2097152 | tf_op jit(solution)/shard_map/psum | solution.py:16
  480.5 134.6 %reduce-scatter.2.cloned.1.call-start = ((), (), s32[]{:S(2)}) async-start(), calls=%async_computation.5 | async-start | bytes 6291456 | tf_op jit(solution)/shard_map/reduce_scatter | solution.py:46
  552.1 439.1 %all-gather.3.cloned.1.call-start = ((), (), s32[]{:S(2)}) async-start(), calls=%async_computation.6 | async-start | bytes 35651584 | tf_op jit(solution)/shard_map/all_gather | solution.py:10
Sparse Core Ops, SparseCore 0:
  12.0 224.5 all-reduce.4
  239.5 60.7 all-reduce.6
  310.6 167.5 all-reduce.8
  481.0 61.0 all-reduce.10
  552.3 62.8 reduce-scatter.1
  617.4 373.7 all-gather.2
